TPU v7x, 128 devices: a whole 4x4x4 slice. The times are simulated.
128 devices in a mesh: gx: 16 (over z, x), gy: 8 (over y, core).
Axes of the slice: x: 4, y: 4, z: 4, core: 2. Of those that a mesh axis runs over, the one named last changes fastest.
Arguments:
- field: float32 [32, 1024, 1024], P(None, 'gx', 'gy'), may hold values from -6 to 6
- conductivity: float32 [32, 1024, 1024], P(None, 'gx', 'gy'), may hold values from 0.2 to 1
- rate: float32 [32, 1024, 1024], P(None, 'gx', 'gy'), may hold values from 0.05 to 0.5
- patch_cell: int32 [32768], P(('gx', 'gy')), may hold values from 0 to 255
- trainer: int32 [32768, 1], P(('gx', 'gy')), may hold values from 0 to 127; in each aligned block of 256 rows (0 to 255, 256 to 511, ...) at most 4 rows name the same one
- res_slot: int32 [131072], P(('gx', 'gy')), may hold values from 0 to 2047
- reservoir: bfloat16 [262144, 2048], P(('gx', 'gy')), may hold values from -6 to 6
- weights: float32 [2, 1024, 1024], P(None, ('gx', 'gy')), may hold values from -0.1875 to 0.1875
- w_mom: float32 [2, 1024, 1024], P(None, ('gx', 'gy')), may hold values from -0.75 to 0.75
- w_var: float32 [2, 1024, 1024], P(None, ('gx', 'gy')), may hold values from 0.001 to 0.1
- biases: float32 [2, 1024], P(None, ('gx', 'gy')), may hold values from -6 to 6
- b_mom: float32 [2, 1024], P(None, ('gx', 'gy')), may hold values from -0.75 to 0.75
- b_var: float32 [2, 1024], P(None, ('gx', 'gy')), may hold values from 0.001 to 2
Outputs:
- new_field: float32 [32, 1024, 1024], P(None, 'gx', 'gy')
- new_weights: float32 [2, 1024, 1024], P(None, ('gx', 'gy'))
- new_w_mom: float32 [2, 1024, 1024], P(None, ('gx', 'gy'))
- new_w_var: float32 [2, 1024, 1024], P(None, ('gx', 'gy'))
- new_biases: float32 [2, 1024], P(None, ('gx', 'gy'))
- new_b_mom: float32 [2, 1024], P(None, ('gx', 'gy'))
- new_b_var: float32 [2, 1024], P(None, ('gx', 'gy'))
Inputs may be any that keep to these rules, and one draw needn't show every extreme that they name: At most 4 of the patches of one device go to one trainer. `res_slot`: slots of the trainer's own reservoir.
All inputs are finite; a program needn't handle non-finite values.
Results may differ from a plain program's by a relative error of at most 0.0003.
The roundings to bfloat16 on the way count: a program that leaves them out, or rounds other values in their place, can miss the bound.
Values may be sent and summed in bfloat16 or wider, within the bound.
No kernel may reach another device: no remote copies, remote signals or barrier semaphores. Data moves between devices by JAX's collectives and lax.ppermute only.
A program may use at most 128 MiB of HBM per device.

v0:
```python
import jax
import jax.numpy as jnp
from jax import lax
from jax.sharding import PartitionSpec as P

PW = 32
STEPS = 4
time_step = 0.15
learn_rate = 0.001
beta_one = 0.9
beta_two = 0.99
adam_count = 20
tiny_eps = 1e-08


def with_halo(x, sides, width):
    for axis, dim in sides:
        peers, length = (lax.axis_size(axis), x.shape[dim])
        up = [(i, (i + 1) % peers) for i in range(peers - 1)]
        down = [(j, i) for i, j in up]
        last = lax.slice_in_dim(x, length - width, length, axis=dim)
        first = lax.slice_in_dim(x, 0, width, axis=dim)
        before = lax.ppermute(last, axis, up)
        after = lax.ppermute(first, axis, down)
        x = jnp.concatenate([before, x, after], axis=dim)
    return x


def update(padded, kpad, rate_inner):
    inner = slice(1, -1)
    centre = padded[1:-1, 1:-1, 1:-1]
    kcentre = kpad[1:-1, 1:-1, 1:-1]
    sides = [
        (slice(2, None), inner, inner),
        (slice(None, -2), inner, inner),
        (inner, slice(2, None), inner),
        (inner, slice(None, -2), inner),
        (inner, inner, slice(2, None)),
        (inner, inner, slice(None, -2)),
    ]
    flux = jnp.zeros_like(centre)
    for where in sides:
        flux = flux + 0.5 * (kcentre + kpad[where]) * (padded[where] - centre)
    return centre + time_step * (flux - rate_inner * centre)


def zpad(array):
    return jnp.pad(array, ((1, 1), (0, 0), (0, 0)))


def local_grads(rows, live, wbf, bbf):
    width = wbf.shape[1]
    inputs = rows[:, :width]
    target = rows[:, width:].astype(jnp.float32)
    pre = jnp.dot(inputs, wbf[0], preferred_element_type=jnp.float32) + bbf[0].astype(jnp.float32)
    hidden = jnp.tanh(pre)
    hidden_b = hidden.astype(jnp.bfloat16)
    pred = jnp.dot(hidden_b, wbf[1], preferred_element_type=jnp.float32) + bbf[1].astype(
        jnp.float32
    )
    count = jnp.sum(live)
    grad_pred = 2.0 * (pred - target) * live[:, None] / count
    grad_pred_b = grad_pred.astype(jnp.bfloat16)
    grad_w2 = jnp.dot(hidden_b.T, grad_pred_b, preferred_element_type=jnp.float32)
    grad_hid = jnp.dot(grad_pred_b, wbf[1].T, preferred_element_type=jnp.float32)
    grad_pre = grad_hid * (1.0 - hidden * hidden)
    grad_pre_b = grad_pre.astype(jnp.bfloat16)
    grad_w1 = jnp.dot(inputs.T, grad_pre_b, preferred_element_type=jnp.float32)
    return (jnp.stack([grad_w1, grad_w2]), jnp.stack([jnp.sum(grad_pre, 0), jnp.sum(grad_pred, 0)]))


def adam(param, moment, second, grad):
    moment_new = beta_one * moment + (1.0 - beta_one) * grad
    second_new = beta_two * second + (1.0 - beta_two) * grad * grad
    mhat = moment_new / (1.0 - beta_one**adam_count)
    vhat = second_new / (1.0 - beta_two**adam_count)
    return (param - learn_rate * mhat / (jnp.sqrt(vhat) + tiny_eps), moment_new, second_new)


def local(
    field,
    conductivity,
    rate,
    patch_cell,
    trainer,
    res_slot,
    reservoir,
    weights,
    w_mom,
    w_var,
    biases,
    b_mom,
    b_var,
):
    depth, cells_x, cells_y = field.shape
    state = field
    kpad = zpad(with_halo(conductivity, (("gx", 1), ("gy", 2)), 1))
    for step in range(STEPS):
        padded = with_halo(state, (("gx", 1), ("gy", 2)), 1)
        state = update(zpad(padded), kpad, rate)
    devices = lax.axis_size("gx") * lax.axis_size("gy")
    count_dev = patch_cell.shape[0]
    cap = max(2, 2 * count_dev // devices)
    stacked = jnp.stack([field, state]).reshape(2, depth, cells_x * cells_y // PW, PW)
    picked = stacked[:, :, patch_cell, :]
    patches = (
        jnp.transpose(picked, (2, 0, 1, 3)).reshape(count_dev, 2 * depth * PW).astype(jnp.bfloat16)
    )
    target_of = trainer[:, 0]
    onehot = (target_of[:, None] == jnp.arange(devices, dtype=jnp.int32)[None, :]).astype(jnp.int32)
    rank = jnp.sum(jnp.cumsum(onehot, 0) * onehot, 1) - 1
    where_to = target_of * cap + rank
    width2 = patches.shape[1]
    outbox = jnp.zeros((devices * cap, width2), jnp.bfloat16).at[where_to].set(patches)
    flags = (
        jnp.zeros((devices * cap,), jnp.bfloat16)
        .at[where_to]
        .set(jnp.ones((count_dev,), jnp.bfloat16))
    )
    arrived, alive = (
        lax.all_to_all(
            outbox.reshape(devices, cap, width2),
            ("gx", "gy"),
            split_axis=0,
            concat_axis=0,
            tiled=True,
        ),
        lax.all_to_all(
            flags.reshape(devices, cap), ("gx", "gy"), split_axis=0, concat_axis=0, tiled=True
        ),
    )
    arrived = arrived.reshape(devices * cap, width2)
    alive = alive.reshape(devices * cap).astype(jnp.float32)
    wfull, bfull = (
        lax.all_gather(weights.astype(jnp.bfloat16), ("gx", "gy"), axis=1, tiled=True),
        lax.all_gather(biases.astype(jnp.bfloat16), ("gx", "gy"), axis=1, tiled=True),
    )
    rows = jnp.concatenate([reservoir[res_slot], arrived], 0)
    live = jnp.concatenate([jnp.ones((res_slot.shape[0],), jnp.float32), alive])
    grad_w, grad_b = local_grads(rows, live, wfull, bfull)
    share_w, share_b = (
        lax.psum_scatter(grad_w, ("gx", "gy"), scatter_dimension=1, tiled=True),
        lax.psum_scatter(grad_b, ("gx", "gy"), scatter_dimension=1, tiled=True),
    )
    new_w, new_wm, new_wv = adam(weights, w_mom, w_var, share_w)
    new_b, new_bm, new_bv = adam(biases, b_mom, b_var, share_b)
    return (state, new_w, new_wm, new_wv, new_b, new_bm, new_bv)


def solution(mesh):
    return jax.shard_map(
        local,
        mesh=mesh,
        in_specs=(
            P(None, "gx", "gy"),
            P(None, "gx", "gy"),
            P(None, "gx", "gy"),
            P(("gx", "gy")),
            P(("gx", "gy"), None),
            P(("gx", "gy")),
            P(("gx", "gy"), None),
            P(None, ("gx", "gy"), None),
            P(None, ("gx", "gy"), None),
            P(None, ("gx", "gy"), None),
            P(None, ("gx", "gy")),
            P(None, ("gx", "gy")),
            P(None, ("gx", "gy")),
        ),
        out_specs=(
            P(None, "gx", "gy"),
            P(None, ("gx", "gy"), None),
            P(None, ("gx", "gy"), None),
            P(None, ("gx", "gy"), None),
            P(None, ("gx", "gy")),
            P(None, ("gx", "gy")),
            P(None, ("gx", "gy")),
        ),
        check_vma=False,
    )
```

profile of v0, /device:TPU:0, one launch (start us, length us, event | category | flops | bytes accessed | tf_op | source)
XLA Modules:
  0.0 1021.7 jit_solution(17814061396416684958)
XLA Ops:
  14.0 4.5 collective-permute-start.4
  34.5 5.4 collective-permute-start.6
  56.2 5.1 fusion.73
  62.7 5.2 collective-permute-start.8
  91.3 5.1 fusion.55
  102.2 4.3 collective-permute-done.13
  124.9 22.5 %all-to-all-start.1 = ((bf16[128,1,4]{2,1,0:T(2,128)(2,1)}), bf16[128,1,4]{2,1,0:T(2,128)(2,1)}, u32[]{:S(2)}, u32[]{:S(2)}) async-start(bf16[128,1,4]{2,1,0:T(2,128)(2,1)} %all_to_all.12), calls=%async_computation.1 | async-start | bytes 131072 | tf_op jit(solution)/shard_map/all_to_all | solution.py:128
  155.5 5.1 fusion.37
  178.0 12.3 %collective-permute-start.19 = (f32[32,66,1]{1,0,2:T(8,128)}, f32[32,66,1]{1,0,2:T(8,128)}, u32[]{:S(2)}, u32[]{:S(2)}) collective-permute-start(f32[32,66,1]{1,0,2:T(8,128)} %copy.255), channel_id=1, source_target_pairs={{1,0},{2,1},{3,2},{4,3},{5,4},{6,5},{7,6},{9,8},{10,9},{11,10},{12... | collective-permute-start | bytes 25352 | tf_op jit(solution)/shard_map/ppermute | solution.py:24
  195.3 4.3 copy.264
  207.7 5.8 fusion.19
  220.7 5.4 gather_fusion.1
  226.2 4.9 copy.266
  236.9 14.4 %all-to-all-start = ((bf16[128,4,2048]{2,1,0:T(4,128)(2,1)}), bf16[128,4,2048]{2,1,0:T(4,128)(2,1)S(1)}, u32[]{:S(2)}, u32[]{:S(2)}) async-start(bf16[128,4,2048]{2,1,0:T(4,128)(2,1)} %reshape.62), calls=%async_computation | async-start | bytes 4194304 | tf_op jit(solution)/shard_map/all_to_all | solution.py:121
  251.4 49.2 %all-gather = bf16[128,8,2]{1,2,0:T(2,128)(2,1)S(1)} all-gather(bf16[1,8,2]{1,2,0:T(2,128)(2,1)S(1)} %convert_bitcast_fusion), channel_id=1, replica_groups=mesh['gx'=16,'gy'=8] {'gx','gy'}, dimensions={0}, use_global_device_ids=true | all-gather | bytes 4128 | tf_op jit(solution)/shard_map/all_gather | solution.py:136
  300.8 13.5 %gather_fusion = bf16[1024,2048]{1,0:T(8,128)(2,1)} fusion(bf16[2048,2048]{1,0:T(8,128)(2,1)} %param.19, s32[1024]{0:T(1024)S(1)} %copy-done.58), kind=kCustom, calls=%fused_computation | custom fusion | bytes 8392704 | tf_op jit(solution)/shard_map/gather | solution.py:138
  314.3 4.8 constant_dynamic-update-slice_fusion.1
  326.1 6.2 fusion.4
  332.3 4.8 fusion.121
  340.7 6.2 fusion.122
  346.8 5.5 fusion.7
  352.4 4.2 pad_maximum_fusion.1
  356.6 64.3 %all-reduce.6 = f32[2,1024]{1,0:T(2,128)S(1)} all-reduce(f32[2,1024]{1,0:T(2,128)S(1)} %pad_maximum_fusion.47), channel_id=3, replica_groups=mesh['gx'=16,'gy'=8] {'gx','gy'}, use_global_device_ids=true, to_apply=%region_9.10.clone | all-reduce | flops 2048 | bytes 16384
  421.6 591.2 %reduce-scatter.3.cloned.1.call-done = f32[2,8,1024]{2,1,0:T(8,128)} async-done(((f32[2,1024,1024]{2,1,0:T(8,128)}), f32[2,8,1024]{2,1,0:T(8,128)}) %reduce-scatter.3.cloned.1.call-update) | async-done | bytes 65552 | tf_op jit(solution)/shard_map/reduce_scatter | solution.py:142
  (252 shorter events, 151.9 us)
Async XLA Ops:
  7.2 318.9 %all-gather.3.cloned.1.call-start = ((), (), s32[]{:S(2)}) async-start(), calls=%async_computation.3 | async-start | bytes 4227072 | tf_op jit(solution)/shard_map/all_gather | solution.py:135
  8.2 14.2 %collective-permute-start = (f32[32,1,128]{2,0,1:T(8,128)S(1)}, f32[32,1,128]{2,0,1:T(8,128)S(1)}, u32[]{:S(2)}, u32[]{:S(2)}) collective-permute-start(f32[32,1,128]{2,0,1:T(8,128)S(1)} %bitcast.121), channel_id=1, source_target_pairs={{0,8},{8,16},{16,24},{24,32},{32,40},{40,48},{48,56},{56,64},{64,7... | collective-permute-start | bytes 49160 | tf_op jit(solution)/shard_map/ppermute | solution.py:23
  11.7 10.7 %collective-permute-start.1 = (f32[32,1,128]{2,0,1:T(8,128)S(1)}, f32[32,1,128]{2,0,1:T(8,128)S(1)}, u32[]{:S(2)}, u32[]{:S(2)}) collective-permute-start(f32[32,1,128]{2,0,1:T(8,128)S(1)} %bitcast.120), channel_id=1, source_target_pairs={{8,0},{16,8},{24,16},{32,24},{40,32},{48,40},{56,48},{64,56},{72,6... | collective-permute-start | bytes 49160 | tf_op jit(solution)/shard_map/ppermute | solution.py:24
  14.0 16.5 %collective-permute-start.4 = (f32[32,1,128]{2,0,1:T(8,128)S(1)}, f32[32,1,128]{2,0,1:T(8,128)S(1)}, u32[]{:S(2)}, u32[]{:S(2)}) collective-permute-start(f32[32,1,128]{2,0,1:T(8,128)S(1)} %bitcast.119), channel_id=1, source_target_pairs={{0,8},{8,16},{16,24},{24,32},{32,40},{40,48},{48,56},{56,64},{64,7... | collective-permute-start | bytes 49160 | tf_op jit(solution)/shard_map/ppermute | solution.py:23
  18.6 12.0 %collective-permute-start.5 = (f32[32,1,128]{2,0,1:T(8,128)S(1)}, f32[32,1,128]{2,0,1:T(8,128)S(1)}, u32[]{:S(2)}, u32[]{:S(2)}) collective-permute-start(f32[32,1,128]{2,0,1:T(8,128)S(1)} %bitcast.118), channel_id=1, source_target_pairs={{8,0},{16,8},{24,16},{32,24},{40,32},{48,40},{56,48},{64,56},{72,6... | collective-permute-start | bytes 49160 | tf_op jit(solution)/shard_map/ppermute | solution.py:24
  27.5 14.8 %collective-permute-start.2 = (f32[32,66,1]{1,0,2:T(8,128)S(1)}, f32[32,66,1]{1,0,2:T(8,128)S(1)}, u32[]{:S(2)}, u32[]{:S(2)}) collective-permute-start(f32[32,66,1]{1,0,2:T(8,128)S(1)} %copy.206), channel_id=1, source_target_pairs={{0,1},{1,2},{2,3},{3,4},{4,5},{5,6},{6,7},{8,9},{9,10},{10,11},{11... | collective-permute-start | bytes 25352 | tf_op jit(solution)/shard_map/ppermute | solution.py:23
  29.2 14.6 %collective-permute-start.3 = (f32[32,66,1]{1,0,2:T(8,128)S(1)}, f32[32,66,1]{1,0,2:T(8,128)S(1)}, u32[]{:S(2)}, u32[]{:S(2)}) collective-permute-start(f32[32,66,1]{1,0,2:T(8,128)S(1)} %copy.207), channel_id=1, source_target_pairs={{1,0},{2,1},{3,2},{4,3},{5,4},{6,5},{7,6},{9,8},{10,9},{11,10},{12... | collective-permute-start | bytes 25352 | tf_op jit(solution)/shard_map/ppermute | solution.py:24
  34.5 13.6 %collective-permute-start.6 = (f32[32,66,1]{1,0,2:T(8,128)}, f32[32,66,1]{1,0,2:T(8,128)}, u32[]{:S(2)}, u32[]{:S(2)}) collective-permute-start(f32[32,66,1]{1,0,2:T(8,128)} %copy.214), channel_id=1, source_target_pairs={{0,1},{1,2},{2,3},{3,4},{4,5},{5,6},{6,7},{8,9},{9,10},{10,11},{11... | collective-permute-start | bytes 25352 | tf_op jit(solution)/shard_map/ppermute | solution.py:23
  41.0 9.4 collective-permute-start.7
  61.4 7.2 collective-permute-start.9
  62.7 6.6 collective-permute-start.8
  74.1 9.0 collective-permute-start.10
  79.9 5.4 collective-permute-start.11
  96.4 5.8 collective-permute-start.12
  100.3 6.2 collective-permute-start.13
  111.3 36.0 %collective-permute-start.14 = (f32[32,66,1]{1,0,2:T(8,128)}, f32[32,66,1]{1,0,2:T(8,128)}, u32[]{:S(2)}, u32[]{:S(2)}) collective-permute-start(f32[32,66,1]{1,0,2:T(8,128)} %copy.242), channel_id=1, source_target_pairs={{0,1},{1,2},{2,3},{3,4},{4,5},{5,6},{6,7},{8,9},{9,10},{10,11},{11... | collective-permute-start | bytes 25352 | tf_op jit(solution)/shard_map/ppermute | solution.py:23
  117.5 32.1 %collective-permute-start.15 = (f32[32,66,1]{1,0,2:T(8,128)}, f32[32,66,1]{1,0,2:T(8,128)}, u32[]{:S(2)}, u32[]{:S(2)}) collective-permute-start(f32[32,66,1]{1,0,2:T(8,128)} %copy.243), channel_id=1, source_target_pairs={{1,0},{2,1},{3,2},{4,3},{5,4},{6,5},{7,6},{9,8},{10,9},{11,10},{12... | collective-permute-start | bytes 25352 | tf_op jit(solution)/shard_map/ppermute | solution.py:24
  124.9 112.1 %all-to-all-start.1 = ((bf16[128,1,4]{2,1,0:T(2,128)(2,1)}), bf16[128,1,4]{2,1,0:T(2,128)(2,1)}, u32[]{:S(2)}, u32[]{:S(2)}) async-start(bf16[128,1,4]{2,1,0:T(2,128)(2,1)} %all_to_all.12), calls=%async_computation.1 | async-start | bytes 131072 | tf_op jit(solution)/shard_map/all_to_all | solution.py:128
  160.6 4.7 collective-permute-start.16
  163.4 5.6 collective-permute-start.17
  173.8 25.7 %collective-permute-start.18 = (f32[32,66,1]{1,0,2:T(8,128)}, f32[32,66,1]{1,0,2:T(8,128)}, u32[]{:S(2)}, u32[]{:S(2)}) collective-permute-start(f32[32,66,1]{1,0,2:T(8,128)} %copy.254), channel_id=1, source_target_pairs={{0,1},{1,2},{2,3},{3,4},{4,5},{5,6},{6,7},{8,9},{9,10},{10,11},{11... | collective-permute-start | bytes 25352 | tf_op jit(solution)/shard_map/ppermute | solution.py:23
  178.0 23.8 %collective-permute-start.19 = (f32[32,66,1]{1,0,2:T(8,128)}, f32[32,66,1]{1,0,2:T(8,128)}, u32[]{:S(2)}, u32[]{:S(2)}) collective-permute-start(f32[32,66,1]{1,0,2:T(8,128)} %copy.255), channel_id=1, source_target_pairs={{1,0},{2,1},{3,2},{4,3},{5,4},{6,5},{7,6},{9,8},{10,9},{11,10},{12... | collective-permute-start | bytes 25352 | tf_op jit(solution)/shard_map/ppermute | solution.py:24
  236.9 83.9 %all-to-all-start = ((bf16[128,4,2048]{2,1,0:T(4,128)(2,1)}), bf16[128,4,2048]{2,1,0:T(4,128)(2,1)S(1)}, u32[]{:S(2)}, u32[]{:S(2)}) async-start(bf16[128,4,2048]{2,1,0:T(4,128)(2,1)} %reshape.62), calls=%async_computation | async-start | bytes 4194304 | tf_op jit(solution)/shard_map/all_to_all | solution.py:121
  251.4 761.5 %reduce-scatter.3.cloned.1.call-start = ((), (), s32[]{:S(2)}) async-start(), calls=%async_computation.4 | async-start | bytes 8454144 | tf_op jit(solution)/shard_map/reduce_scatter | solution.py:142
  (67 other events, 2431.5 us)
Sparse Core Ops, SparseCore 0:
  21.5 72.0 all-gather.2
  356.7 656.1 reduce-scatter.2
where the time goes:
time: 1030 us; the launch traced here: 1020 us
  waiting for transfers between devices  600 us (58%)
  blocking collectives  114 us (11%)
  local copies, waits for them, and re-layouts  113 us (11%)
  starting transfers between devices  96.9 us (9%)
  other arithmetic  56.5 us (5%)
  matrix products  26.3 us (3%)
  between operations  15.5 us (2%)
    reduce_scatter x1, waiting for transfers between devices, local(): lax.psum_scatter(grad_w, ('gx', 'gy'), scatter_dimension=1, tiled=True)  591 us
    unnamed x1, blocking collectives  64.3 us
    all_gather x1, blocking collectives, local(): lax.all_gather(biases.astype(jnp.bfloat16), ('gx', 'gy'), axis=1, tiled=T...  49.2 us
    ppermute x10, starting transfers between devices, with_halo(): before = lax.ppermute(last, axis, up)  35.8 us
    ppermute x10, starting transfers between devices, with_halo(): after = lax.ppermute(first, axis, down)  24.1 us
    all_to_all x1, starting transfers between devices, local(): lax.all_to_all(flags.reshape(devices, cap), ('gx', 'gy'), split_axis=0, c...  22.5 us
    add x4, other arithmetic, update(): return centre + time_step * (flux - rate_inner * centre)  21 us
  transfers between devices with their start and end apart: 24, of which 4 were waited for; matrix products, arithmetic and copies ran while one was open for 15% of the time, Pallas kernels for 0%

commit v1 on v0

--- a/solution.py
+++ b/solution.py
@@ -133,7 +133,15 @@
     alive = alive.reshape(devices * cap).astype(jnp.float32)
     wfull, bfull = (
         lax.all_gather(weights.astype(jnp.bfloat16), ("gx", "gy"), axis=1, tiled=True),
-        lax.all_gather(biases.astype(jnp.bfloat16), ("gx", "gy"), axis=1, tiled=True),
+        jnp.concatenate(
+            lax.all_to_all(
+                jnp.stack([biases.astype(jnp.bfloat16)] * lax.axis_size(("gx", "gy"))),
+                ("gx", "gy"),
+                0,
+                0,
+            ),
+            axis=1,
+        ),
     )
     rows = jnp.concatenate([reservoir[res_slot], arrived], 0)
     live = jnp.concatenate([jnp.ones((res_slot.shape[0],), jnp.float32), alive])

time: 1030 us -> 984 us (0.955)
  blocking collectives: 114 us -> 63.2 us
    all_gather x1 -> x0, blocking collectives: 49.2 us -> none  [local(): lax.all_gather(biases.astype(jnp.bfloat16), ('gx', 'gy'), axis=1, tiled=T...]
    all_to_all x0 -> x1, starting transfers between devices: none -> 14.4 us  [local(): lax.all_to_all(jnp.stack([biases.astype(jnp.bfloat16)] * lax.axis_size(('...]
    ppermute x10, starting transfers between devices: 24.1 us -> 13.5 us  [with_halo(): after = lax.ppermute(first, axis, down)]
  transfers between devices with their start and end apart: 24 -> 25, of which waited for: 4 -> 5; matrix products, arithmetic and copies ran while one was open for 15% -> 16% of each run, Pallas kernels for 0% -> 0%
where the time goes in v1:
time: 984 us; the launch traced here: 975 us
  waiting for transfers between devices  607 us (62%)
  local copies, waits for them, and re-layouts  110 us (11%)
  starting transfers between devices  96.2 us (10%)
  blocking collectives  63.2 us (6%)
  other arithmetic  59.6 us (6%)
  matrix products  23.1 us (2%)
  between operations  15.3 us (2%)
    reduce_scatter x1, waiting for transfers between devices, local(): lax.psum_scatter(grad_w, ('gx', 'gy'), scatter_dimension=1, tiled=True)  589 us
    unnamed x1, blocking collectives  63.2 us
    ppermute x10, starting transfers between devices, with_halo(): before = lax.ppermute(last, axis, up)  36 us
    all_to_all x1, starting transfers between devices, local(): lax.all_to_all(flags.reshape(devices, cap), ('gx', 'gy'), split_axis=0, c...  22.3 us
    add x4, other arithmetic, update(): return centre + time_step * (flux - rate_inner * centre)  21.1 us
  transfers between devices with their start and end apart: 25, of which 5 were waited for; matrix products, arithmetic and copies ran while one was open for 16% of the time, Pallas kernels for 0%

profile of v1, /device:TPU:0, one launch (start us, length us, event | category | flops | bytes accessed | tf_op | source)
XLA Modules:
  0.0 974.8 jit_solution(16518857602788616627)
XLA Ops:
  14.0 4.5 collective-permute-start.4
  30.6 5.4 collective-permute-start.6
  52.4 5.1 fusion.73
  58.8 5.2 collective-permute-start.8
  86.7 5.1 fusion.55
  98.0 4.3 collective-permute-done.13
  120.6 22.3 %all-to-all-start.2 = ((bf16[128,1,4]{2,1,0:T(2,128)(2,1)}), bf16[128,1,4]{2,1,0:T(2,128)(2,1)}, u32[]{:S(2)}, u32[]{:S(2)}) async-start(bf16[128,1,4]{2,1,0:T(2,128)(2,1)} %all_to_all.16), calls=%async_computation.2 | async-start | bytes 131072 | tf_op jit(solution)/shard_map/all_to_all | solution.py:128
  151.1 5.1 fusion.37
  179.8 4.3 copy.259
  192.8 5.8 fusion.19
  204.8 14.4 %all-to-all-start.1 = ((bf16[128,2,8]{2,1,0:T(2,128)(2,1)}), bf16[128,2,8]{2,1,0:T(2,128)(2,1)S(1)}, u32[]{:S(2)}, u32[]{:S(2)}) async-start(bf16[128,2,8]{2,1,0:T(2,128)(2,1)} %stack.23), calls=%async_computation.1 | async-start | bytes 131072 | tf_op jit(solution)/shard_map/all_to_all | solution.py:137
  219.2 5.2 pad_maximum_fusion
  224.4 5.5 gather_fusion.1
  229.9 4.9 copy.261
  240.6 9.8 %all-to-all-start = ((bf16[128,4,2048]{2,1,0:T(4,128)(2,1)}), bf16[128,4,2048]{2,1,0:T(4,128)(2,1)S(1)}, u32[]{:S(2)}, u32[]{:S(2)}) async-start(bf16[128,4,2048]{2,1,0:T(4,128)(2,1)} %reshape.86), calls=%async_computation | async-start | bytes 4194304 | tf_op jit(solution)/shard_map/all_to_all | solution.py:121
  250.6 13.3 %gather_fusion = bf16[1024,2048]{1,0:T(8,128)(2,1)} fusion(bf16[2048,2048]{1,0:T(8,128)(2,1)} %param.19, s32[1024]{0:T(1024)S(1)} %copy-done.57), kind=kCustom, calls=%fused_computation | custom fusion | bytes 8392704 | tf_op jit(solution)/shard_map/gather | solution.py:146
  263.9 4.8 constant_dynamic-update-slice_fusion.1
  271.0 9.7 all-to-all-done
  286.0 6.2 fusion.4
  292.2 4.8 fusion.123
  300.6 5.0 fusion.124
  309.2 4.2 pad_maximum_fusion.1
  313.4 63.2 %all-reduce.6 = f32[2,1024]{1,0:T(2,128)S(1)} all-reduce(f32[2,1024]{1,0:T(2,128)S(1)} %pad_maximum_fusion.47), channel_id=3, replica_groups=mesh['gx'=16,'gy'=8] {'gx','gy'}, use_global_device_ids=true, to_apply=%region_9.10.clone | all-reduce | flops 2048 | bytes 16384
  377.4 588.9 %reduce-scatter.3.cloned.1.call-done = f32[2,8,1024]{2,1,0:T(8,128)} async-done(((f32[2,1024,1024]{2,1,0:T(8,128)}), f32[2,8,1024]{2,1,0:T(8,128)}) %reduce-scatter.3.cloned.1.call-update) | async-done | bytes 65552 | tf_op jit(solution)/shard_map/reduce_scatter | solution.py:150
  (256 shorter events, 152.6 us)
Async XLA Ops:
  7.2 278.9 %all-gather.2.cloned.1.call-start = ((), (), s32[]{:S(2)}) async-start(), calls=%async_computation.4 | async-start | bytes 4227072 | tf_op jit(solution)/shard_map/all_gather | solution.py:135
  8.2 14.9 %collective-permute-start = (f32[32,1,128]{2,0,1:T(8,128)S(1)}, f32[32,1,128]{2,0,1:T(8,128)S(1)}, u32[]{:S(2)}, u32[]{:S(2)}) collective-permute-start(f32[32,1,128]{2,0,1:T(8,128)S(1)} %bitcast.113), channel_id=1, source_target_pairs={{0,8},{8,16},{16,24},{24,32},{32,40},{40,48},{48,56},{56,64},{64,7... | collective-permute-start | bytes 49160 | tf_op jit(solution)/shard_map/ppermute | solution.py:23
  11.7 11.3 %collective-permute-start.1 = (f32[32,1,128]{2,0,1:T(8,128)S(1)}, f32[32,1,128]{2,0,1:T(8,128)S(1)}, u32[]{:S(2)}, u32[]{:S(2)}) collective-permute-start(f32[32,1,128]{2,0,1:T(8,128)S(1)} %bitcast.112), channel_id=1, source_target_pairs={{8,0},{16,8},{24,16},{32,24},{40,32},{48,40},{56,48},{64,56},{72,6... | collective-permute-start | bytes 49160 | tf_op jit(solution)/shard_map/ppermute | solution.py:24
  14.0 14.9 %collective-permute-start.4 = (f32[32,1,128]{2,0,1:T(8,128)S(1)}, f32[32,1,128]{2,0,1:T(8,128)S(1)}, u32[]{:S(2)}, u32[]{:S(2)}) collective-permute-start(f32[32,1,128]{2,0,1:T(8,128)S(1)} %bitcast.111), channel_id=1, source_target_pairs={{0,8},{8,16},{16,24},{24,32},{32,40},{40,48},{48,56},{56,64},{64,7... | collective-permute-start | bytes 49160 | tf_op jit(solution)/shard_map/ppermute | solution.py:23
  18.6 10.3 %collective-permute-start.5 = (f32[32,1,128]{2,0,1:T(8,128)S(1)}, f32[32,1,128]{2,0,1:T(8,128)S(1)}, u32[]{:S(2)}, u32[]{:S(2)}) collective-permute-start(f32[32,1,128]{2,0,1:T(8,128)S(1)} %bitcast.110), channel_id=1, source_target_pairs={{8,0},{16,8},{24,16},{32,24},{40,32},{48,40},{56,48},{64,56},{72,6... | collective-permute-start | bytes 49160 | tf_op jit(solution)/shard_map/ppermute | solution.py:24
  25.9 12.5 %collective-permute-start.2 = (f32[32,66,1]{1,0,2:T(8,128)S(1)}, f32[32,66,1]{1,0,2:T(8,128)S(1)}, u32[]{:S(2)}, u32[]{:S(2)}) collective-permute-start(f32[32,66,1]{1,0,2:T(8,128)S(1)} %copy.201), channel_id=1, source_target_pairs={{0,1},{1,2},{2,3},{3,4},{4,5},{5,6},{6,7},{8,9},{9,10},{10,11},{11... | collective-permute-start | bytes 25352 | tf_op jit(solution)/shard_map/ppermute | solution.py:23
  27.6 12.3 %collective-permute-start.3 = (f32[32,66,1]{1,0,2:T(8,128)S(1)}, f32[32,66,1]{1,0,2:T(8,128)S(1)}, u32[]{:S(2)}, u32[]{:S(2)}) collective-permute-start(f32[32,66,1]{1,0,2:T(8,128)S(1)} %copy.202), channel_id=1, source_target_pairs={{1,0},{2,1},{3,2},{4,3},{5,4},{6,5},{7,6},{9,8},{10,9},{11,10},{12... | collective-permute-start | bytes 25352 | tf_op jit(solution)/shard_map/ppermute | solution.py:24
  30.6 13.6 %collective-permute-start.6 = (f32[32,66,1]{1,0,2:T(8,128)}, f32[32,66,1]{1,0,2:T(8,128)}, u32[]{:S(2)}, u32[]{:S(2)}) collective-permute-start(f32[32,66,1]{1,0,2:T(8,128)} %copy.209), channel_id=1, source_target_pairs={{0,1},{1,2},{2,3},{3,4},{4,5},{5,6},{6,7},{8,9},{9,10},{10,11},{11... | collective-permute-start | bytes 25352 | tf_op jit(solution)/shard_map/ppermute | solution.py:23
  37.1 9.4 collective-permute-start.7
  57.5 7.2 collective-permute-start.9
  58.8 6.6 collective-permute-start.8
  69.7 8.8 collective-permute-start.10
  75.4 5.4 collective-permute-start.11
  91.9 6.0 collective-permute-start.12
  96.1 6.2 collective-permute-start.13
  107.1 35.8 %collective-permute-start.14 = (f32[32,66,1]{1,0,2:T(8,128)}, f32[32,66,1]{1,0,2:T(8,128)}, u32[]{:S(2)}, u32[]{:S(2)}) collective-permute-start(f32[32,66,1]{1,0,2:T(8,128)} %copy.237), channel_id=1, source_target_pairs={{0,1},{1,2},{2,3},{3,4},{4,5},{5,6},{6,7},{8,9},{9,10},{10,11},{11... | collective-permute-start | bytes 25352 | tf_op jit(solution)/shard_map/ppermute | solution.py:23
  113.3 31.9 %collective-permute-start.15 = (f32[32,66,1]{1,0,2:T(8,128)}, f32[32,66,1]{1,0,2:T(8,128)}, u32[]{:S(2)}, u32[]{:S(2)}) collective-permute-start(f32[32,66,1]{1,0,2:T(8,128)} %copy.238), channel_id=1, source_target_pairs={{1,0},{2,1},{3,2},{4,3},{5,4},{6,5},{7,6},{9,8},{10,9},{11,10},{12... | collective-permute-start | bytes 25352 | tf_op jit(solution)/shard_map/ppermute | solution.py:24
  120.6 83.5 %all-to-all-start.2 = ((bf16[128,1,4]{2,1,0:T(2,128)(2,1)}), bf16[128,1,4]{2,1,0:T(2,128)(2,1)}, u32[]{:S(2)}, u32[]{:S(2)}) async-start(bf16[128,1,4]{2,1,0:T(2,128)(2,1)} %all_to_all.16), calls=%async_computation.2 | async-start | bytes 131072 | tf_op jit(solution)/shard_map/all_to_all | solution.py:128
  159.0 5.6 collective-permute-start.17
  168.9 15.7 %collective-permute-start.18 = (f32[32,66,1]{1,0,2:T(8,128)}, f32[32,66,1]{1,0,2:T(8,128)}, u32[]{:S(2)}, u32[]{:S(2)}) collective-permute-start(f32[32,66,1]{1,0,2:T(8,128)} %copy.249), channel_id=1, source_target_pairs={{0,1},{1,2},{2,3},{3,4},{4,5},{5,6},{6,7},{8,9},{9,10},{10,11},{11... | collective-permute-start | bytes 25352 | tf_op jit(solution)/shard_map/ppermute | solution.py:23
  173.1 13.8 %collective-permute-start.19 = (f32[32,66,1]{1,0,2:T(8,128)}, f32[32,66,1]{1,0,2:T(8,128)}, u32[]{:S(2)}, u32[]{:S(2)}) collective-permute-start(f32[32,66,1]{1,0,2:T(8,128)} %copy.250), channel_id=1, source_target_pairs={{1,0},{2,1},{3,2},{4,3},{5,4},{6,5},{7,6},{9,8},{10,9},{11,10},{12... | collective-permute-start | bytes 25352 | tf_op jit(solution)/shard_map/ppermute | solution.py:24
  204.8 35.8 %all-to-all-start.1 = ((bf16[128,2,8]{2,1,0:T(2,128)(2,1)}), bf16[128,2,8]{2,1,0:T(2,128)(2,1)S(1)}, u32[]{:S(2)}, u32[]{:S(2)}) async-start(bf16[128,2,8]{2,1,0:T(2,128)(2,1)} %stack.23), calls=%async_computation.1 | async-start | bytes 131072 | tf_op jit(solution)/shard_map/all_to_all | solution.py:137
  240.6 40.1 %all-to-all-start = ((bf16[128,4,2048]{2,1,0:T(4,128)(2,1)}), bf16[128,4,2048]{2,1,0:T(4,128)(2,1)S(1)}, u32[]{:S(2)}, u32[]{:S(2)}) async-start(bf16[128,4,2048]{2,1,0:T(4,128)(2,1)} %reshape.86), calls=%async_computation | async-start | bytes 4194304 | tf_op jit(solution)/shard_map/all_to_all | solution.py:121
  250.4 715.8 %reduce-scatter.3.cloned.1.call-start = ((), (), s32[]{:S(2)}) async-start(), calls=%async_computation.5 | async-start | bytes 8454144 | tf_op jit(solution)/shard_map/reduce_scatter | solution.py:150
  (69 other events, 2423.0 us)
Sparse Core Ops, SparseCore 0:
  21.5 72.0 all-gather.1
  313.5 652.6 reduce-scatter.2
